TPU v7x, 32 devices: a whole 2x2x4 slice. The times are simulated.
32 devices in a mesh: rows: 16 (over z, y, x), heads: 2 (over core).
Axes of the slice: x: 2, y: 2, z: 4, core: 2. Of those that a mesh axis runs over, the one named last changes fastest.
Arguments:
- tokens: bfloat16 [32768, 768], P(('rows', 'heads')), may hold values from -6 to 6
- cotangent: bfloat16 [32768, 768], P(('rows', 'heads')), may hold values from -6 to 6
- segment_ids: int32 [64, 512], P('rows'), may hold values from 0 to 7, never falling along the last dimension, each value on 1 to 256 neighbouring positions
- valid_count: int32 [64], P('rows'), may hold values from 1 to 512, 24576 in all
- qkv_weight: bfloat16 [768, 2304], P(('rows', 'heads')), may hold values from -0.21875 to 0.21875
- qv_bias: bfloat16 [2, 768], P(None, ('rows', 'heads')), may hold values from -0.59765625 to 0.59765625
- out_weight: bfloat16 [768, 768], P(('rows', 'heads')), may hold values from -1.75 to 1.75
- out_bias: bfloat16 [768], P(('rows', 'heads')), may hold values from -1.796875 to 1.796875
- norm_gain: bfloat16 [768], P(('rows', 'heads')), may hold values from 0.5 to 1.5
- norm_shift: bfloat16 [768], P(('rows', 'heads')), may hold values from -1.796875 to 1.796875
- in_weight: bfloat16 [768, 3072], P(('rows', 'heads')), may hold values from -0.21875 to 0.21875
- in_bias: bfloat16 [3072], P(('rows', 'heads')), may hold values from -1.796875 to 1.796875
- back_weight: bfloat16 [3072, 768], P(('rows', 'heads')), may hold values from -0.109375 to 0.109375
- back_bias: bfloat16 [768], P(('rows', 'heads')), may hold values from -1.796875 to 1.796875
- final_gain: bfloat16 [768], P(('rows', 'heads')), may hold values from 0.5 to 1.5
- final_shift: bfloat16 [768], P(('rows', 'heads')), may hold values from -1.796875 to 1.796875
Outputs:
- layer_out: bfloat16 [32768, 768], P(('rows', 'heads'))
- grad_tokens: float32 [32768, 768], P(('rows', 'heads'))
- grad_qkv_weight: float32 [768, 2304], P(('rows', 'heads'))
- grad_qv_bias: float32 [2, 768], P(None, ('rows', 'heads'))
- grad_out_weight: float32 [768, 768], P(('rows', 'heads'))
- grad_out_bias: float32 [768], P(('rows', 'heads'))
- grad_norm_gain: float32 [768], P(('rows', 'heads'))
- grad_norm_shift: float32 [768], P(('rows', 'heads'))
- grad_in_weight: float32 [768, 3072], P(('rows', 'heads'))
- grad_in_bias: float32 [3072], P(('rows', 'heads'))
- grad_back_weight: float32 [3072, 768], P(('rows', 'heads'))
- grad_back_bias: float32 [768], P(('rows', 'heads'))
- grad_final_gain: float32 [768], P(('rows', 'heads'))
- grad_final_shift: float32 [768], P(('rows', 'heads'))
Inputs may be any that keep to these rules, and one draw needn't show every extreme that they name: `segment_ids`: along a row the numbers never fall; each segment spans 1 to 256 positions. `valid_count`: the counts of all 64 rows sum to 24576.
All inputs are finite; a program needn't handle non-finite values. No bound on the sum of `valid_count` on one device may be relied on, other than what follows from the above.
Results may differ from a plain program's by a relative error of at most 0.013.
Values may be sent and summed in bfloat16 or wider, within the bound.
No kernel may reach another device: no remote copies, remote signals or barrier semaphores. Data moves between devices by JAX's collectives and lax.ppermute only.
A program may use at most 192 MiB of HBM per device.

v0:
```python
import math
import jax
import jax.numpy as jnp
from jax import lax
from jax.sharding import PartitionSpec as P

HEADS = 12
HEAD_DIM = 64
EPS = 1e-12
AXES = ("rows", "heads")
F32 = jnp.float32
BF16 = jnp.bfloat16


def norm_forward(values, gain_row, shift_row):
    centered = values - jnp.mean(values, axis=-1, keepdims=True)
    inverse = lax.rsqrt(jnp.mean(centered * centered, axis=-1, keepdims=True) + EPS)
    normalized = centered * inverse
    return (normalized * gain_row + shift_row, normalized, inverse)


def norm_backward(grad_output, normalized, inverse, gain_row):
    grad_normed = grad_output * gain_row
    grad_input = inverse * (
        grad_normed
        - jnp.mean(grad_normed, axis=-1, keepdims=True)
        - normalized * jnp.mean(grad_normed * normalized, axis=-1, keepdims=True)
    )
    return (grad_input, jnp.sum(grad_output * normalized, axis=0), jnp.sum(grad_output, axis=0))


def allowed_keys(segment_row, count_row):
    positions = jnp.arange(segment_row.shape[0])
    same_segment = segment_row[:, None] == segment_row[None, :]
    return same_segment & (positions[None, :] < count_row) | (
        positions[:, None] == positions[None, :]
    )


def masked_scores(query_rows, key_rows, allowed):
    scores = jnp.einsum(
        "qhd,khd->hqk", query_rows, key_rows, preferred_element_type=F32
    ) * HEAD_DIM ** (-0.5)
    return jnp.where(allowed[None], scores, -1e30)


def attend_forward(query_rows, key_rows, value_rows, segment_row, count_row):
    scores = masked_scores(query_rows, key_rows, allowed_keys(segment_row, count_row))
    highest = jnp.max(scores, axis=-1, keepdims=True)
    exponent = jnp.exp(scores - highest)
    total = jnp.sum(exponent, axis=-1, keepdims=True)
    low = (exponent / total).astype(BF16)
    context = jnp.einsum("hqk,khd->qhd", low, value_rows, preferred_element_type=F32)
    return (context.astype(BF16), (highest + jnp.log(total))[..., 0])


def attend_backward(query_rows, key_rows, value_rows, segment_row, count_row, lse, grad_context):
    scores = masked_scores(query_rows, key_rows, allowed_keys(segment_row, count_row))
    soft = jnp.exp(scores - lse[..., None])
    low = soft.astype(BF16)
    grad_value = jnp.einsum("hqk,qhd->khd", low, grad_context, preferred_element_type=F32)
    grad_soft = jnp.einsum("qhd,khd->hqk", grad_context, value_rows, preferred_element_type=F32)
    inner = jnp.sum(soft * grad_soft, axis=-1, keepdims=True)
    grad_scores = (soft * (grad_soft - inner)).astype(BF16)
    scaling = HEAD_DIM ** (-0.5)
    grad_query = (
        jnp.einsum("hqk,khd->qhd", grad_scores, key_rows, preferred_element_type=F32) * scaling
    )
    grad_key = (
        jnp.einsum("hqk,qhd->khd", grad_scores, query_rows, preferred_element_type=F32) * scaling
    )
    return tuple((g.astype(BF16) for g in (grad_query, grad_key, grad_value)))


def local(
    tokens,
    cotangent,
    segment_ids,
    valid_count,
    qkv_weight,
    qv_bias,
    out_weight,
    out_bias,
    norm_gain,
    norm_shift,
    in_weight,
    in_bias,
    back_weight,
    back_bias,
    final_gain,
    final_shift,
):
    head_index = lax.axis_index("heads")
    devices = lax.axis_size("rows") * lax.axis_size("heads")
    token_count, width = tokens.shape
    row_length = segment_ids.shape[1]
    rows = token_count // row_length
    shard = qkv_weight.shape[0]
    small = [
        qv_bias[0],
        qv_bias[1],
        out_bias,
        norm_gain,
        norm_shift,
        in_bias,
        back_bias,
        final_gain,
        final_shift,
    ]
    sizes = [s.shape[0] for s in small]
    total = sum(sizes)
    lanes = -(-total // (shard * 128)) * 128
    packed = jnp.pad(jnp.concatenate(small), (0, shard * lanes - total)).reshape(shard, lanes)
    first = lax.all_gather(jnp.concatenate([qkv_weight, packed], axis=1), AXES, axis=0, tiled=True)
    qkv_all = first[:, : 3 * width]
    vectors = first[:, 3 * width :].reshape(devices, shard * lanes)
    parts = []
    at = 0
    for n in sizes:
        parts.append(vectors[:, at : at + n].reshape(devices * n).astype(F32))
        at += n
    q_bias, v_bias, out_bias_f, gain_f, shift_f, in_bias_f, back_bias_f, fgain_f, fshift_f = parts
    second = lax.all_gather(
        jnp.concatenate([out_weight, in_weight], axis=1), AXES, axis=0, tiled=True
    )
    out_all = second[:, :width]
    in_all = second[:, width:]
    back_all = lax.all_gather(back_weight, AXES, axis=0, tiled=True)
    segments = lax.dynamic_slice(segment_ids, (head_index * rows, 0), (rows, row_length))
    counts = lax.dynamic_slice(valid_count, (head_index * rows,), (rows,))
    bias_full = jnp.concatenate([q_bias, jnp.zeros_like(q_bias), v_bias])
    projected = (jnp.dot(tokens, qkv_all, preferred_element_type=F32) + bias_full).astype(BF16)
    heads = projected.reshape(rows, row_length, 3, HEADS, HEAD_DIM)
    contexts = [
        attend_forward(heads[r, :, 0], heads[r, :, 1], heads[r, :, 2], segments[r], counts[r])
        for r in range(rows)
    ]
    context = jnp.concatenate([c[0].reshape(row_length, width) for c in contexts], axis=0)
    valid = (jnp.arange(row_length)[None, :] < counts[:, None]).astype(F32).reshape(token_count, 1)
    attn = jnp.dot(context, out_all, preferred_element_type=F32) + out_bias_f
    hidden, n1, r1 = norm_forward(tokens.astype(F32) + attn, gain_f, shift_f)
    hidden_low = hidden.astype(BF16)
    preact = jnp.dot(hidden_low, in_all, preferred_element_type=F32) + in_bias_f
    cdf = 0.5 + 0.5 * lax.erf(preact * 0.5**0.5)
    activation = (preact * cdf).astype(BF16)
    slope = (
        cdf + preact * jnp.exp(-0.5 * preact * preact) * (1.0 / math.sqrt(2 * math.pi))
    ).astype(BF16)
    feed = jnp.dot(activation, back_all, preferred_element_type=F32) + back_bias_f
    finished, n2, r2 = norm_forward(hidden + feed, fgain_f, fshift_f)
    layer_out = (finished * valid).astype(BF16)
    grad_final = cotangent.astype(F32) * valid
    g_res2, g_fgain, g_fshift = norm_backward(grad_final, n2, r2, fgain_f)
    g_ffn = g_res2.astype(BF16)
    g_back_bias = jnp.sum(g_ffn.astype(F32), axis=0)
    g_back = jnp.einsum("tf,td->fd", activation, g_ffn, preferred_element_type=F32).astype(BF16)
    g_back = lax.psum_scatter(g_back, AXES, scatter_dimension=0, tiled=True)
    g_act = jnp.einsum("td,fd->tf", g_ffn, back_all, preferred_element_type=F32)
    g_pre = (g_act * slope.astype(F32)).astype(BF16)
    g_in_bias = jnp.sum(g_pre.astype(F32), axis=0)
    g_in = jnp.einsum("td,tf->df", hidden_low, g_pre, preferred_element_type=F32).astype(BF16)
    g_hidden = g_res2 + jnp.einsum("tf,df->td", g_pre, in_all, preferred_element_type=F32)
    g_res1, g_gain, g_shift = norm_backward(g_hidden, n1, r1, gain_f)
    g_attn = g_res1.astype(BF16)
    g_out_bias = jnp.sum(g_attn.astype(F32), axis=0)
    g_out = jnp.einsum("tc,td->cd", context, g_attn, preferred_element_type=F32).astype(BF16)
    g_oi = lax.psum_scatter(
        jnp.concatenate([g_out, g_in], axis=1), AXES, scatter_dimension=0, tiled=True
    )
    g_context = jnp.einsum("td,cd->tc", g_attn, out_all, preferred_element_type=F32).astype(BF16)
    g_heads = g_context.reshape(rows, row_length, HEADS, HEAD_DIM)
    grads = [
        attend_backward(
            heads[r, :, 0],
            heads[r, :, 1],
            heads[r, :, 2],
            segments[r],
            counts[r],
            contexts[r][1],
            g_heads[r],
        )
        for r in range(rows)
    ]
    g_proj = jnp.concatenate(
        [jnp.concatenate([g.reshape(row_length, width) for g in row], axis=1) for row in grads],
        axis=0,
    )
    g_qkv = jnp.einsum("td,tc->dc", tokens, g_proj, preferred_element_type=F32).astype(BF16)
    sums = jnp.sum(g_proj.astype(F32), axis=0).reshape(3, width)
    g_small = [
        sums[0],
        sums[2],
        g_out_bias,
        g_gain,
        g_shift,
        g_in_bias,
        g_back_bias,
        g_fgain,
        g_fshift,
    ]
    g_packed = jnp.concatenate([g.reshape(devices, -1) for g in g_small], axis=1)
    g_packed = jnp.pad(g_packed, ((0, 0), (0, shard * lanes - total))).astype(BF16)
    g_last = lax.psum_scatter(
        jnp.concatenate([g_qkv, g_packed.reshape(devices * shard, lanes)], axis=1),
        AXES,
        scatter_dimension=0,
        tiled=True,
    )
    grad_tokens = g_res1 + jnp.einsum("tc,dc->td", g_proj, qkv_all, preferred_element_type=F32)
    mine = g_last[:, 3 * width :].reshape(shard * lanes).astype(F32)
    own = []
    at = 0
    for n in sizes:
        own.append(mine[at : at + n])
        at += n
    return (
        layer_out,
        grad_tokens,
        g_last[:, : 3 * width].astype(F32),
        jnp.stack([own[0], own[1]]),
        g_oi[:, :width].astype(F32),
        own[2],
        own[3],
        own[4],
        g_oi[:, width:].astype(F32),
        own[5],
        g_back.astype(F32),
        own[6],
        own[7],
        own[8],
    )


def solution(mesh):
    both = P(AXES, None)
    vec = P(AXES)
    in_specs = (
        both,
        both,
        P("rows", None),
        P("rows"),
        both,
        P(None, AXES),
        both,
        vec,
        vec,
        vec,
        both,
        vec,
        both,
        vec,
        vec,
        vec,
    )
    out_specs = (
        both,
        both,
        both,
        P(None, AXES),
        both,
        vec,
        vec,
        vec,
        both,
        vec,
        both,
        vec,
        vec,
        vec,
    )
    return jax.shard_map(local, mesh=mesh, in_specs=in_specs, out_specs=out_specs, check_vma=False)
```

profile of v0, /device:TPU:0, one launch (start us, length us, event | category | flops | bytes accessed | tf_op | source)
XLA Modules:
  0.0 740.3 jit_solution(17252090711581574381)
XLA Ops:
  8.0 4.8 concatenate.34
  19.6 1.7 copy.88
  23.5 54.4 %all-gather.4.cloned.1.call-done = bf16[768,2432]{1,0:T(8,128)(2,1)} async-done(((bf16[24,2432]{1,0:T(8,128)(2,1)}), bf16[768,2432]{1,0:T(8,128)(2,1)}) %all-gather.4.cloned.1.call-update) | async-done | bytes 3735568 | tf_op jit(solution)/shard_map/all_gather | solution.py:114
  79.2 9.0 %fusion.17 = bf16[1024,2304]{0,1:T(8,128)(2,1)} fusion(bf16[1024,768]{1,0:T(8,128)(2,1)} %param.16, f32[2304]{0:T(1024)S(1)} %pad_maximum_fusion.7, bf16[768,2432]{1,0:T(8,128)(2,1)} %all-gather.4.cloned.1.call-done), kind=kOutput, calls=%fused_computation.36 | convolution fusion | flops 3628597248 | bytes 9839616 | tf_op jit(solution)/shard_map/dot_general | solution.py:132
  88.2 8.8 %reshape.390 = bf16[2,512,3,12,64]{1,0,4,3,2:T(2,128)(2,1)} reshape(bf16[1024,2304]{0,1:T(8,128)(2,1)} %fusion.17) | data formatting | bytes 9437184 | tf_op jit(solution)/shard_map/reshape | solution.py:133
  97.1 12.6 %fusion.72 = (bf16[1,512,1,12,64]{1,0,4,3,2:T(2,128)(2,1)}, bf16[1,512,1,12,64]{1,0,4,3,2:T(2,128)(2,1)S(1)}, bf16[1,512,1,12,64]{1,0,4,3,2:T(2,128)(2,1)}, bf16...) fusion(bf16[2,512,3,12,64]{1,0,4,3,2:T(2,128)(2,1)} %reshape.390), kind=kLoop, calls=%fused_computation.152 | loop fusion | bytes 9437184 | tf_op jit(solution)/shard_map/slice | solution.py:135
  109.7 2.1 fusion.20
  111.8 2.6 fusion.6
  114.4 1.9 copy-done
  117.1 9.1 %fusion.19 = (f32[12,512]{1,0:T(8,128)S(1)}, f32[12,512,512]{1,2,0:T(8,128)}) fusion(pred[512,512]{0,1:T(8,128)(4,1)S(1)} %fusion.47, bf16[1,512,1,12,64]{1,0,4,3,2:T(2,128)(2,1)} %get-tuple-element.71, bf16[1,512,1,12,64]{1,0,4,3,2:T(2,128)(2,1)} %get-tuple-element.72), kind=kOutput, calls=%fused_computation.39 | convolution fusion | flops 412084224 | bytes 14442496 | tf_op jit(solution)/shard_map/qhd,khd->hqk/dot_general | solution.py:41
  126.2 7.3 fusion.5
  133.6 5.9 fusion.44
  139.5 4.5 fusion.45
  144.0 3.7 all-gather.6.cloned.1.call-done
  147.7 3.7 fusion.77
  153.1 11.3 %multiply_convert_fusion.3 = (bf16[1024,3072]{1,0:T(8,128)(2,1)}, f32[1024,3072]{1,0:T(8,128)}) fusion(f32[3072]{0:T(1024)S(1)} %reshape.412, bf16[768,3840]{1,0:T(8,128)(2,1)S(1)} %copy-done.31, f32[1024,768]{0,1:T(8,128)S(1)} %get-tuple-element.106, f32[768]{0:T(1024)S(1)} %reshape.411, f32[768]{0:T(1024)S(1)} %reshape.410, ...), kind=kOutput, calls=%fused_computation.13 | convolution fusion | flops 4854644736 | bytes 26767360 | tf_op jit(solution)/shard_map/dot_general | solution.py:143
  164.4 48.5 %all-gather.8.cloned.1.call-done = bf16[3072,768]{1,0:T(8,128)(2,1)} async-done(((bf16[96,768]{1,0:T(8,128)(2,1)}), bf16[3072,768]{1,0:T(8,128)(2,1)}) %all-gather.8.cloned.1.call-update) | async-done | bytes 4718608 | tf_op jit(solution)/shard_map/all_gather | solution.py:128
  212.9 9.4 %fusion.78 = (f32[1024]{0:T(1024)S(1)}, f32[1024,768]{0,1:T(8,128)S(1)}) fusion(f32[768]{0:T(1024)S(1)} %reshape.413, bf16[1024,3072]{1,0:T(8,128)(2,1)} %get-tuple-element.107, bf16[3072,768]{1,0:T(8,128)(2,1)} %all-gather.8.cloned.1.call-done, f32[768]{0:T(1024)S(1)} %reshape.411, f32[768]{0:T(1024)S(1)} %reshape.410, f32[1024]{0:T(1024)S(1)} %add_rsqrt_fusion.1, ...), kind=kOutput, calls=%fused_computation.158 | convolution fusion | flops 4837342208 | bytes 17323008 | tf_op jit(solution)/shard_map/dot_general | solution.py:149
  222.8 3.8 multiply_reduce_fusion.2
  226.6 2.0 fusion.70
  228.6 16.2 %fusion.79 = (bf16[3072]{0:T(1024)(128)(2,1)}, bf16[1024,3072]{1,0:T(8,128)(2,1)}) fusion(f32[1024,3072]{1,0:T(8,128)} %get-tuple-element.108, f32[3072]{0:T(1024)S(1)} %reshape.412, bf16[1024,768]{0,1:T(8,128)(2,1)S(1)} %get-tuple-element.65, bf16[3072,768]{1,0:T(8,128)(2,1)S(1)} %bitcast.142), kind=kOutput, calls=%fused_computation.159 | convolution fusion | flops 4875875328 | bytes 25184256 | tf_op jit(solution)/shard_map/td,fd->tf/dot_general | solution.py:158
  244.9 11.4 %multiply_reduce_fusion.3 = (bf16[768]{0:T(1024)(128)(2,1)}, f32[1024]{0:T(1024)S(1)}, f32[1024]{0:T(1024)S(1)}, bf16[768]{0:T(1024)(128)(2,1)}, f32[1024,768]{0,1:T(8,128)S(1)}) fusion(f32[1024,768]{0,1:T(8,128)S(1)} %copy-done.3, f32[1024]{0:T(1024)S(1)} %add_rsqrt_fusion.1, f32[1024]{0:T(1024)S(1)} %broadcast_multiply_fusion.5, f32[768]{0:T(1024)S(1)} %reshape.410, ...), kind=kOutput, calls=%fused_computation.47 | convolution fusion | flops 4846776320 | bytes 22066176 | tf_op jit(solution)/shard_map/tf,df->td/dot_general | solution.py:162
  256.3 1.7 convert_reduce_fusion
  258.0 3.6 convolution_convert_fusion.3
  261.7 4.0 fusion.38
  265.7 8.4 %multiply_reduce_fusion.1 = (f32[12,512]{1,0:T(8,128)S(1)}, f32[12,512,512]{1,2,0:T(8,128)}) fusion(f32[12,512]{1,0:T(8,128)S(1)} %log_add_fusion.1, f32[12,512,512]{1,2,0:T(8,128)S(1)} %bitcast.113, pred[512,512]{0,1:T(8,128)(4,1)S(1)} %fusion.47, bf16[512,12,64]{0,2,1:T(8,128)(2,1)S(1)} %bitcast.117, bf16[1,512,1,12,64]{1,0,4,3,2:T(2,128)(2,1)} %get-tuple-element.68), kind=kOutput, calls=%fused_computation.10 | convolution fusion | flops 418375680 | bytes 27049984 | tf_op jit(solution)/shard_map/qhd,khd->hqk/dot_general | solution.py:62
  274.1 10.3 %multiply_convert_fusion.1 = bf16[12,512,512]{1,2,0:T(8,128)(2,1)S(1)} fusion(f32[12,512,512]{1,2,0:T(8,128)} %get-tuple-element.115, f32[12,512]{1,0:T(8,128)S(1)} %get-tuple-element.114, f32[12,512]{1,0:T(8,128)S(1)} %log_add_fusion.1, f32[12,512,512]{1,2,0:T(8,128)} %get-tuple-element.104, pred[512,512]{0,1:T(8,128)(4,1)S(1)} %fusion.47), kind=kLoop, calls=%fused_computation.9 | loop fusion | flops 18874368 | bytes 31768576 | tf_op jit(solution)/shard_map/convert_element_type | solution.py:64
  284.4 2.0 multiply_convert_fusion.7
  287.6 3.2 fusion.41
  290.8 7.1 multiply_reduce_fusion
  297.9 7.1 multiply_convert_fusion
  305.0 2.0 multiply_convert_fusion.5
  310.4 28.5 %fusion.18 = bf16[768,2304]{0,1:T(8,128)(2,1)S(1)} fusion(bf16[1024,768]{1,0:T(8,128)(2,1)S(1)} %copy-done.21, bf16[512,768]{0,1:T(8,128)(2,1)S(1)} %bitcast.134, bf16[512,768]{0,1:T(8,128)(2,1)S(1)} %bitcast.125, bf16[512,768]{0,1:T(8,128)(2,1)S(1)} %bitcast.128, bf16[512,768]{0,1:T(8,128)(2,1)S(1)} %bitcast.132, bf16[512,768]{0,1:T(8,128)(2,1)S(1)} %bitcast.119, ...), kind=kOutput, calls=%fused_computation.38 | convolution fusion | flops 3653959680 | bytes 9830400 | tf_op jit(solution)/shard_map/td,tc->dc/dot_general | solution.py:188
  354.8 1.7 reshape.406
  356.5 1.7 copy.97
  358.2 3.1 pad_maximum_fusion.1
  362.7 10.0 %convolution_convert_fusion = bf16[3072,768]{1,0:T(8,128)(2,1)} fusion(bf16[1024,3072]{1,0:T(8,128)(2,1)} %get-tuple-element.107, bf16[1024,768]{0,1:T(8,128)(2,1)S(1)} %copy-done.23), kind=kOutput, calls=%fused_computation.33 | convolution fusion | flops 4834197504 | bytes 12582912 | tf_op jit(solution)/shard_map/tf,td->fd/dot_general | solution.py:156
  372.8 5.0 convolution_convert_fusion.4
  377.8 2.6 copy.99
  380.4 8.5 %convolution_convert_fusion.1 = bf16[768,3072]{1,0:T(8,128)(2,1)S(1)} fusion(bf16[1024,3072]{1,0:T(8,128)(2,1)} %get-tuple-element.117, f32[1024,768]{0,1:T(8,128)S(1)} %copy-done.4, f32[768]{0:T(1024)S(1)} %copy-done.29, f32[768]{0:T(1024)S(1)} %reshape.410, f32[1024]{0:T(1024)S(1)} %copy-done.27, f32[1024]{0:T(1024)S(1)} %broadcast_multiply_fusion.5), kind=kOutput, calls=%fused_computation.34 | convolution fusion | flops 4838129664 | bytes 14170112 | tf_op jit(solution)/shard_map/td,tf->df/dot_general | solution.py:161
  388.9 2.9 pad_maximum_fusion
  394.8 8.3 %fusion.32 = f32[1024,768]{0,1:T(8,128)S(1)} fusion(f32[1024,768]{0,1:T(8,128)} %copy-done.15, bf16[768,2432]{1,0:T(8,128)(2,1)} %all-gather.4.cloned.1.call-done, bf16[512,768]{0,1:T(8,128)(2,1)} %bitcast.135, bf16[512,768]{0,1:T(8,128)(2,1)} %bitcast.126, bf16[512,768]{0,1:T(8,128)(2,1)} %bitcast.129, bf16[512,768]{0,1:T(8,128)(2,1)} %bitcast.130, ...), kind=kOutput, calls=%fused_computation.71 | convolution fusion | flops 3652976640 | bytes 14548992 | tf_op jit(solution)/shard_map/tc,dc->td/dot_general | solution.py:209
  403.2 2.4 copy.101
  405.5 94.7 %all-reduce.5.cloned.1.call-done = bf16[768,2432]{0,1:T(8,128)(2,1)} async-done(((bf16[768,2432]{0,1:T(8,128)(2,1)}), bf16[768,2432]{0,1:T(8,128)(2,1)}) %all-reduce.5.cloned.1.call-update) | async-done | bytes 3735568
  505.6 106.8 %reduce-scatter.6.cloned.1.call-done = bf16[96,768]{1,0:T(8,128)(2,1)} async-done(((bf16[3072,768]{1,0:T(8,128)(2,1)}), bf16[96,768]{1,0:T(8,128)(2,1)}) %reduce-scatter.6.cloned.1.call-update) | async-done | bytes 147472 | tf_op jit(solution)/shard_map/reduce_scatter | solution.py:157
  612.4 1.6 convert_element_type.316
  614.0 116.2 %reduce-scatter.4.cloned.1.call-done = bf16[24,3840]{1,0:T(8,128)(2,1)} async-done(((bf16[768,3840]{1,0:T(8,128)(2,1)}), bf16[24,3840]{1,0:T(8,128)(2,1)}) %reduce-scatter.4.cloned.1.call-update) | async-done | bytes 184336 | tf_op jit(solution)/shard_map/reduce_scatter | solution.py:167
  731.6 1.6 slice_convert_fusion
  (171 shorter events, 45.4 us)
Async XLA Ops:
  7.2 14.1 %copy-start.20 = (bf16[1024,768]{1,0:T(8,128)(2,1)S(1)}, bf16[1024,768]{1,0:T(8,128)(2,1)}, u32[]{:S(2)}) copy-start(bf16[1024,768]{1,0:T(8,128)(2,1)} %param.16) | copy-start | bytes 4718596
  7.2 15.7 %copy-start.30 = (s32[4,512]{1,0:T(4,128)S(1)}, s32[4,512]{1,0:T(4,128)}, u32[]{:S(2)}) copy-start(s32[4,512]{1,0:T(4,128)} %param.18) | copy-start | bytes 24580
  7.2 70.7 %all-gather.4.cloned.1.call-start = ((), (), s32[]{:S(2)}) async-start(), calls=%async_computation.2 | async-start | bytes 3852288 | tf_op jit(solution)/shard_map/all_gather | solution.py:114
  14.4 133.3 %all-gather.6.cloned.1.call-start = ((), (), s32[]{:S(2)}) async-start(), calls=%async_computation.3 | async-start | bytes 6082560 | tf_op jit(solution)/shard_map/all_gather | solution.py:123
  16.1 196.8 %all-gather.8.cloned.1.call-start = ((), (), s32[]{:S(2)}) async-start(), calls=%async_computation.4 | async-start | bytes 4866048 | tf_op jit(solution)/shard_map/all_gather | solution.py:128
  16.8 483.4 %all-reduce.5.cloned.1.call-start = ((), (), s32[]{:S(2)}) async-start(), calls=%async_computation.7 | async-start | bytes 7471104
  109.6 2.2 copy-start.5
  109.6 2.2 copy-start.7
  111.8 4.5 copy-start
  116.8 96.1 %copy-start.28 = (f32[768]{0:T(1024)}, f32[768]{0:T(1024)S(1)}, u32[]{:S(2)}) copy-start(f32[768]{0:T(1024)S(1)} %reshape.411) | copy-start | bytes 9220
  117.0 16.5 %slice-start = ((s8[12582912]{0:T(1024)(128)(4,1)}), s8[4194304]{0:T(1024)(128)(4,1)S(1)}, s32[]{:S(2)}) async-start(s8[12582912]{0:T(1024)(128)(4,1)} %bitcast.108), calls=%async_computation.8 | async-start | bytes 8388608
  117.0 16.5 %slice-start.1 = ((s8[12582912]{0:T(1024)(128)(4,1)}), s8[4194304]{0:T(1024)(128)(4,1)S(1)}, s32[]{:S(2)}) async-start(s8[12582912]{0:T(1024)(128)(4,1)} %bitcast.108), calls=%async_computation.9 | async-start | bytes 8388608
  126.2 7.4 slice-start.2
  133.6 5.9 copy-start.1
  133.6 5.9 copy-start.14
  139.5 8.3 %copy-start.32 = (bf16[12,64,512]{2,1,0:T(8,128)(2,1)S(1)}, bf16[12,64,512]{2,1,0:T(8,128)(2,1)}, u32[]{:S(2)}) copy-start(bf16[12,64,512]{2,1,0:T(8,128)(2,1)} %fusion.44) | copy-start | bytes 2359300
  147.7 5.4 copy-start.31
  151.5 1.7 copy-start.2
  153.1 103.1 %copy-start.26 = (f32[1024]{0:T(1024)}, f32[1024]{0:T(1024)S(1)}, u32[]{:S(2)}) copy-start(f32[1024]{0:T(1024)S(1)} %add_rsqrt_fusion.1) | copy-start | bytes 12292
  222.3 6.2 slice-start.9
  222.8 5.8 slice-start.10
  228.6 16.3 %copy-start.22 = (bf16[1024,768]{0,1:T(8,128)(2,1)}, bf16[1024,768]{0,1:T(8,128)(2,1)S(1)}, u32[]{:S(2)}) copy-start(bf16[1024,768]{0,1:T(8,128)(2,1)S(1)} %get-tuple-element.65) | copy-start | bytes 4718596
  228.6 16.3 %copy-start.3 = (f32[1024,768]{0,1:T(8,128)S(1)}, f32[1024,768]{0,1:T(8,128)}, u32[]{:S(2)}) copy-start(f32[1024,768]{0,1:T(8,128)} %copy-done.2) | copy-start | bytes 9437188
  228.6 33.1 %slice-start.6 = ((s8[12582912]{0:T(1024)(128)(4,1)}), s8[4194304]{0:T(1024)(128)(4,1)S(1)}, s32[]{:S(2)}) async-start(s8[12582912]{0:T(1024)(128)(4,1)} %bitcast.112), calls=%async_computation.14 | async-start | bytes 8388608
  228.6 33.1 %slice-start.7 = ((s8[12582912]{0:T(1024)(128)(4,1)}), s8[4194304]{0:T(1024)(128)(4,1)S(1)}, s32[]{:S(2)}) async-start(s8[12582912]{0:T(1024)(128)(4,1)} %bitcast.112), calls=%async_computation.15 | async-start | bytes 8388608
  244.9 16.8 %slice-start.8 = ((s8[12582912]{0:T(1024)(128)(4,1)}), s8[4194304]{0:T(1024)(128)(4,1)S(1)}, s32[]{:S(2)}) async-start(s8[12582912]{0:T(1024)(128)(4,1)} %bitcast.112), calls=%async_computation.16 | async-start | bytes 8388608
  258.0 3.7 copy-start.15
  265.7 21.9 %slice-start.3 = ((s8[12582912]{0:T(1024)(128)(4,1)}), s8[4194304]{0:T(1024)(128)(4,1)S(1)}, s32[]{:S(2)}) async-start(s8[12582912]{0:T(1024)(128)(4,1)} %bitcast.110), calls=%async_computation.11 | async-start | bytes 8388608
  265.7 21.9 %slice-start.4 = ((s8[12582912]{0:T(1024)(128)(4,1)}), s8[4194304]{0:T(1024)(128)(4,1)S(1)}, s32[]{:S(2)}) async-start(s8[12582912]{0:T(1024)(128)(4,1)} %bitcast.110), calls=%async_computation.12 | async-start | bytes 8388608
  274.1 10.3 %copy-start.10 = (bf16[1,512,1,12,64]{1,0,4,3,2:T(2,128)(2,1)S(1)}, bf16[1,512,1,12,64]{1,0,4,3,2:T(2,128)(2,1)}, u32[]{:S(2)}) copy-start(bf16[1,512,1,12,64]{1,0,4,3,2:T(2,128)(2,1)} %get-tuple-element.72) | copy-start | bytes 2359300
  274.1 13.5 %slice-start.5 = ((s8[12582912]{0:T(1024)(128)(4,1)}), s8[4194304]{0:T(1024)(128)(4,1)S(1)}, s32[]{:S(2)}) async-start(s8[12582912]{0:T(1024)(128)(4,1)} %bitcast.110), calls=%async_computation.13 | async-start | bytes 8388608
  284.4 2.0 copy-start.9
  286.4 24.0 %copy-start.16 = (bf16[12,64,512]{2,1,0:T(8,128)(2,1)}, bf16[12,64,512]{2,1,0:T(8,128)(2,1)S(1)}, u32[]{:S(2)}) copy-start(bf16[12,64,512]{2,1,0:T(8,128)(2,1)S(1)} %multiply_convert_fusion.7) | copy-start | bytes 2359300
  287.6 22.9 %copy-start.17 = (bf16[12,64,512]{2,1,0:T(8,128)(2,1)}, bf16[12,64,512]{2,1,0:T(8,128)(2,1)S(1)}, u32[]{:S(2)}) copy-start(bf16[12,64,512]{2,1,0:T(8,128)(2,1)S(1)} %multiply_convert_fusion.8) | copy-start | bytes 2359300
  287.6 3.2 copy-start.13
  290.8 19.6 %copy-start.25 = (bf16[12,64,512]{2,1,0:T(8,128)(2,1)}, bf16[12,64,512]{2,1,0:T(8,128)(2,1)S(1)}, u32[]{:S(2)}) copy-start(bf16[12,64,512]{2,1,0:T(8,128)(2,1)S(1)} %fusion.41) | copy-start | bytes 2359300
  297.9 7.1 copy-start.8
  305.0 2.0 copy-start.6
  307.0 3.4 copy-start.18
  308.2 30.8 %copy-start.19 = (bf16[12,64,512]{2,1,0:T(8,128)(2,1)}, bf16[12,64,512]{2,1,0:T(8,128)(2,1)S(1)}, u32[]{:S(2)}) copy-start(bf16[12,64,512]{2,1,0:T(8,128)(2,1)S(1)} %multiply_convert_fusion.6) | copy-start | bytes 2359300
  308.2 2.2 copy-start.21
  361.3 251.0 %reduce-scatter.6.cloned.1.call-start = ((), (), s32[]{:S(2)}) async-start(), calls=%async_computation.6 | async-start | bytes 4866048 | tf_op jit(solution)/shard_map/reduce_scatter | solution.py:157
  372.7 7.7 %copy-start.4 = (f32[1024,768]{0,1:T(8,128)S(1)}, f32[1024,768]{0,1:T(8,128)}, u32[]{:S(2)}) copy-start(f32[1024,768]{0,1:T(8,128)} %copy-done.2) | copy-start | bytes 9437188
  372.7 7.7 %copy-start.27 = (f32[1024]{0:T(1024)S(1)}, f32[1024]{0:T(1024)}, u32[]{:S(2)}) copy-start(f32[1024]{0:T(1024)} %copy-done.26) | copy-start | bytes 12292
  372.7 7.7 %copy-start.29 = (f32[768]{0:T(1024)S(1)}, f32[768]{0:T(1024)}, u32[]{:S(2)}) copy-start(f32[768]{0:T(1024)} %copy-done.28) | copy-start | bytes 9220
  372.7 357.5 %reduce-scatter.4.cloned.1.call-start = ((), (), s32[]{:S(2)}) async-start(), calls=%async_computation.5 | async-start | bytes 6082560 | tf_op jit(solution)/shard_map/reduce_scatter | solution.py:167
  380.4 8.5 %copy-start.12 = (bf16[768,768]{1,0:T(8,128)(2,1)S(1)}, bf16[768,768]{1,0:T(8,128)(2,1)}, u32[]{:S(2)}) copy-start(bf16[768,768]{1,0:T(8,128)(2,1)} %copy.99) | copy-start | bytes 3538948
  391.8 1.4 copy-start.11
  (2 other events, 2.8 us)
Sparse Core Ops, SparseCore 0:
  14.5 63.3 all-gather.3
  81.3 66.3 all-gather.5
  150.6 62.2 all-gather.7
  361.5 138.7 all-reduce.4
  505.6 106.7 reduce-scatter.5
  617.9 112.3 reduce-scatter.3
where the time goes:
time: 748 us; the launch traced here: 740 us
  waiting for transfers between devices  425 us (57%)
  matrix products  176 us (24%)
  local copies, waits for them, and re-layouts  68.1 us (9%)
  other arithmetic  56.3 us (8%)
  between operations  15.1 us (2%)
    reduce_scatter x1, waiting for transfers between devices, local(): lax.psum_scatter(jnp.concatenate([g_out, g_in], axis=1), AXES, scatter_di...  116 us
    reduce_scatter x1, waiting for transfers between devices, local(): g_back = lax.psum_scatter(g_back, AXES, scatter_dimension=0, tiled=True)  107 us
    unnamed x7, waiting for transfers between devices  95.5 us
    all_gather x1, waiting for transfers between devices, local(): lax.all_gather(jnp.concatenate([qkv_weight, packed], axis=1), AXES, axis=...  54.4 us
    all_gather x1, waiting for transfers between devices, local(): back_all = lax.all_gather(back_weight, AXES, axis=0, tiled=True)  48.5 us
    dot_general x1, matrix products, local(): jnp.einsum('td,tc->dc', tokens, g_proj, preferred_element_type=F32)  28.5 us
    convert_element_type x2, other arithmetic, attend_backward(): grad_scores = (soft * (grad_soft - inner)).astype(BF16)  17.4 us
    dot_general x1, matrix products, local(): g_act = jnp.einsum('td,fd->tf', g_ffn, back_all, preferred_element_type=F32)  16.2 us
  transfers between devices with their start and end apart: 6, of which 6 were waited for; matrix products, arithmetic and copies ran while one was open for 18% of the time, Pallas kernels for 0%

commit v1 on v0

--- a/solution.py
+++ b/solution.py
@@ -10,6 +10,28 @@
 AXES = ("rows", "heads")
 F32 = jnp.float32
 BF16 = jnp.bfloat16
+
+
+def joined_along(parts, dim):
+    dims = list(parts.shape[1:])
+    dims[dim] *= parts.shape[0]
+    return jnp.moveaxis(parts, 0, dim).reshape(dims)
+
+
+def collected_by_bits(shard, axis):
+    size = lax.axis_size(axis)
+    blocks = shard[None]
+    for level in range(size.bit_length() - 1):
+        bit = 1 << level
+        theirs = lax.ppermute(blocks, axis, [(i, i ^ bit) for i in range(size)])
+        both = jnp.stack([blocks, theirs])
+        upper = lax.axis_index(axis) >> level & 1
+        blocks = jnp.where(upper == 0, both, both[::-1]).reshape(-1, *shard.shape)
+    return blocks
+
+
+def gather_by_bits(value, axis, dim):
+    return joined_along(collected_by_bits(value, axis), dim)
 
 
 def norm_forward(values, gain_row, shift_row):
@@ -111,7 +133,7 @@
     total = sum(sizes)
     lanes = -(-total // (shard * 128)) * 128
     packed = jnp.pad(jnp.concatenate(small), (0, shard * lanes - total)).reshape(shard, lanes)
-    first = lax.all_gather(jnp.concatenate([qkv_weight, packed], axis=1), AXES, axis=0, tiled=True)
+    first = gather_by_bits(jnp.concatenate([qkv_weight, packed], axis=1), AXES, 0)
     qkv_all = first[:, : 3 * width]
     vectors = first[:, 3 * width :].reshape(devices, shard * lanes)
     parts = []

time: 748 us -> 787 us (1.052)
  waiting for transfers between devices: 425 us -> 449 us
  starting transfers between devices: 0.24 us -> 12.9 us
    ppermute x0 -> x5, waiting for transfers between devices: none -> 130 us  [collected_by_bits(): theirs = lax.ppermute(blocks, axis, [(i, i ^ bit) for i in range(size)])]
    all_gather x1 -> x0, waiting for transfers between devices: 54.4 us -> none  [local(): lax.all_gather(jnp.concatenate([qkv_weight, packed], axis=1), AXES, axis=...]
    all_gather x1, waiting for transfers between devices: 48.5 us -> 0.01 us  [local(): back_all = lax.all_gather(back_weight, AXES, axis=0, tiled=True)]
    ppermute x0 -> x5, starting transfers between devices: none -> 12.7 us  [collected_by_bits(): theirs = lax.ppermute(blocks, axis, [(i, i ^ bit) for i in range(size)])]
    unnamed x95 -> x113, local copies, waits for them, and re-layouts: 14.7 us -> 21.2 us
    unnamed x7 -> x6, waiting for transfers between devices: 95.5 us -> 95.4 us
  transfers between devices with their start and end apart: 6 -> 10, of which waited for: 6 -> 8; matrix products, arithmetic and copies ran while one was open for 18% -> 18% of each run, Pallas kernels for 0% -> 0%
where the time goes in v1:
time: 787 us; the launch traced here: 779 us
  waiting for transfers between devices  449 us (57%)
  matrix products  173 us (22%)
  local copies, waits for them, and re-layouts  72.9 us (9%)
  other arithmetic  55.9 us (7%)
  between operations  14.9 us (2%)
  starting transfers between devices  12.9 us (2%)
    ppermute x5, waiting for transfers between devices, collected_by_bits(): theirs = lax.ppermute(blocks, axis, [(i, i ^ bit) for i in range(size)])  130 us
    reduce_scatter x1, waiting for transfers between devices, local(): lax.psum_scatter(jnp.concatenate([g_out, g_in], axis=1), AXES, scatter_di...  116 us
    reduce_scatter x1, waiting for transfers between devices, local(): g_back = lax.psum_scatter(g_back, AXES, scatter_dimension=0, tiled=True)  107 us
    unnamed x6, waiting for transfers between devices  95.4 us
    dot_general x1, matrix products, local(): jnp.einsum('td,tc->dc', tokens, g_proj, preferred_element_type=F32)  22.6 us
    unnamed x113, local copies, waits for them, and re-layouts  21.2 us
    dot_general x2, matrix products, attend_backward(): jnp.einsum('qhd,khd->hqk', grad_context, value_rows, preferred_element_ty...  18.3 us
    dot_general x1, matrix products, local(): g_act = jnp.einsum('td,fd->tf', g_ffn, back_all, preferred_element_type=F32)  16.3 us
  transfers between devices with their start and end apart: 10, of which 8 were waited for; matrix products, arithmetic and copies ran while one was open for 18% of the time, Pallas kernels for 0%

profile of v1, /device:TPU:0, one launch (start us, length us, event | category | flops | bytes accessed | tf_op | source)
XLA Modules:
  0.0 778.6 jit_solution(10830606625853384599)
XLA Ops:
  9.6 4.8 concatenate.34
  16.9 2.9 collective-permute-start.1
  19.8 6.8 collective-permute-done.1
  26.8 2.3 collective-permute-start.2
  29.1 9.1 %collective-permute-done.2 = bf16[4,24,2432]{2,1,0:T(8,128)(2,1)S(1)} collective-permute-done((bf16[4,24,2432]{2,1,0:T(8,128)(2,1)S(1)}, bf16[4,24,2432]{2,1,0:T(8,128)(2,1)S(1)}, u32[]{:S(2)}, u32[]{:S(2)}) %collective-permute-start.2) | collective-permute-done | bytes 466976 | tf_op jit(solution)/shard_map/ppermute | solution.py:26
  40.2 28.0 %collective-permute-done.3 = bf16[8,24,2432]{2,1,0:T(8,128)(2,1)S(1)} collective-permute-done((bf16[8,24,2432]{2,1,0:T(8,128)(2,1)S(1)}, bf16[8,24,2432]{2,1,0:T(8,128)(2,1)S(1)}, u32[]{:S(2)}, u32[]{:S(2)}) %collective-permute-start.3) | collective-permute-done | bytes 933920 | tf_op jit(solution)/shard_map/ppermute | solution.py:26
  68.7 5.2 collective-permute-start.4
  81.5 85.1 %collective-permute-done.4 = bf16[16,24,2432]{2,1,0:T(8,128)(2,1)} collective-permute-done((bf16[16,24,2432]{2,1,0:T(8,128)(2,1)S(1)}, bf16[16,24,2432]{2,1,0:T(8,128)(2,1)}, u32[]{:S(2)}, u32[]{:S(2)}) %collective-permute-start.4) | collective-permute-done | bytes 1867808 | tf_op jit(solution)/shard_map/ppermute | solution.py:26
  171.4 8.2 %fusion.17 = bf16[1024,2304]{0,1:T(8,128)(2,1)} fusion(bf16[1024,768]{1,0:T(8,128)(2,1)S(1)} %copy-done.28, f32[2304]{0:T(1024)S(1)} %pad_maximum_fusion.12, bf16[768,2432]{1,0:T(8,128)(2,1)} %bitcast.137), kind=kOutput, calls=%fused_computation.37 | convolution fusion | flops 3628597248 | bytes 9839616 | tf_op jit(solution)/shard_map/dot_general | solution.py:154
  179.6 8.8 %reshape.406 = bf16[2,512,3,12,64]{1,0,4,3,2:T(2,128)(2,1)} reshape(bf16[1024,2304]{0,1:T(8,128)(2,1)} %fusion.17) | data formatting | bytes 9437184 | tf_op jit(solution)/shard_map/reshape | solution.py:155
  188.5 12.5 %fusion.76 = (bf16[1,512,1,12,64]{1,0,4,3,2:T(2,128)(2,1)}, bf16[1,512,1,12,64]{1,0,4,3,2:T(2,128)(2,1)}, bf16[1,512,1,12,64]{1,0,4,3,2:T(2,128)(2,1)}, bf16[1,5...) fusion(bf16[2,512,3,12,64]{1,0,4,3,2:T(2,128)(2,1)} %reshape.406), kind=kLoop, calls=%fused_computation.166 | loop fusion | bytes 9437184 | tf_op jit(solution)/shard_map/slice | solution.py:157
  201.0 2.1 fusion.19
  203.2 2.6 fusion.5
  208.4 8.8 %fusion.20 = (f32[12,512]{1,0:T(8,128)S(1)}, f32[12,512,512]{1,2,0:T(8,128)}) fusion(pred[512,512]{0,1:T(8,128)(4,1)S(1)} %copy-done.5, bf16[1,512,1,12,64]{1,0,4,3,2:T(2,128)(2,1)} %get-tuple-element.73, bf16[1,512,1,12,64]{1,0,4,3,2:T(2,128)(2,1)} %get-tuple-element.69), kind=kOutput, calls=%fused_computation.41 | convolution fusion | flops 412084224 | bytes 14442496 | tf_op jit(solution)/shard_map/qhd,khd->hqk/dot_general | solution.py:63
  217.2 7.3 fusion.6
  224.6 5.9 fusion.45
  230.4 4.5 fusion.44
  234.9 3.7 fusion.81
  240.3 11.1 %multiply_convert_fusion.3 = (bf16[1024,3072]{1,0:T(8,128)(2,1)}, f32[1024,3072]{1,0:T(8,128)}) fusion(f32[3072]{0:T(1024)S(1)} %reshape.428, bf16[768,3840]{1,0:T(8,128)(2,1)S(1)} %copy-done.39, f32[1024,768]{0,1:T(8,128)S(1)} %get-tuple-element.110, f32[768]{0:T(1024)S(1)} %reshape.427, f32[768]{0:T(1024)S(1)} %reshape.426, ...), kind=kOutput, calls=%fused_computation.13 | convolution fusion | flops 4854644736 | bytes 26767360 | tf_op jit(solution)/shard_map/dot_general | solution.py:165
  251.4 9.4 %fusion.82 = (f32[1024]{0:T(1024)S(1)}, f32[1024,768]{0,1:T(8,128)S(1)}) fusion(f32[768]{0:T(1024)S(1)} %reshape.429, bf16[1024,3072]{1,0:T(8,128)(2,1)} %get-tuple-element.111, bf16[3072,768]{1,0:T(8,128)(2,1)} %all-gather.5.cloned.1.call-done, f32[768]{0:T(1024)S(1)} %reshape.427, f32[768]{0:T(1024)S(1)} %reshape.426, f32[1024]{0:T(1024)S(1)} %add_rsqrt_fusion.1, ...), kind=kOutput, calls=%fused_computation.172 | convolution fusion | flops 4837342208 | bytes 17323008 | tf_op jit(solution)/shard_map/dot_general | solution.py:171
  261.3 3.8 multiply_reduce_fusion.2
  265.1 2.0 fusion.74
  267.1 16.3 %fusion.83 = (bf16[3072]{0:T(1024)(128)(2,1)}, bf16[1024,3072]{1,0:T(8,128)(2,1)}) fusion(f32[1024,3072]{1,0:T(8,128)} %get-tuple-element.112, f32[3072]{0:T(1024)S(1)} %reshape.428, bf16[1024,768]{0,1:T(8,128)(2,1)S(1)} %get-tuple-element.65, bf16[3072,768]{1,0:T(8,128)(2,1)S(1)} %bitcast.175), kind=kOutput, calls=%fused_computation.173 | convolution fusion | flops 4875875328 | bytes 25184256 | tf_op jit(solution)/shard_map/td,fd->tf/dot_general | solution.py:180
  283.4 11.4 %multiply_reduce_fusion.3 = (bf16[768]{0:T(1024)(128)(2,1)}, f32[1024]{0:T(1024)S(1)}, f32[1024]{0:T(1024)S(1)}, bf16[768]{0:T(1024)(128)(2,1)}, f32[1024,768]{0,1:T(8,128)S(1)}) fusion(f32[1024,768]{0,1:T(8,128)S(1)} %copy-done.3, f32[1024]{0:T(1024)S(1)} %add_rsqrt_fusion.1, f32[1024]{0:T(1024)S(1)} %broadcast_multiply_fusion.5, f32[768]{0:T(1024)S(1)} %reshape.426, ...), kind=kOutput, calls=%fused_computation.49 | convolution fusion | flops 4846776320 | bytes 22066176 | tf_op jit(solution)/shard_map/tf,df->td/dot_general | solution.py:184
  298.2 2.8 convolution_convert_fusion.3
  301.2 7.1 multiply_reduce_fusion.1
  308.3 7.5 multiply_convert_fusion.1
  315.8 2.0 multiply_convert_fusion.8
  317.8 2.9 multiply_convert_fusion.7
  320.8 3.9 fusion.38
  324.7 11.2 %multiply_reduce_fusion = (f32[12,512]{1,0:T(8,128)S(1)}, f32[12,512,512]{1,2,0:T(8,128)}) fusion(f32[12,512]{1,0:T(8,128)S(1)} %log_add_fusion, f32[12,512,512]{1,2,0:T(8,128)} %get-tuple-element.106, pred[512,512]{0,1:T(8,128)(4,1)S(1)} %copy-done.5, bf16[512,12,64]{0,2,1:T(8,128)(2,1)S(1)} %bitcast.141, bf16[1,512,1,12,64]{1,0,4,3,2:T(2,128)(2,1)S(1)} %copy-done.17), kind=kOutput, calls=%fused_computation.7 | convolution fusion | flops 418375680 | bytes 27049984 | tf_op jit(solution)/shard_map/qhd,khd->hqk/dot_general | solution.py:84
  337.3 7.1 multiply_convert_fusion
  344.5 2.0 multiply_convert_fusion.6
  346.5 2.0 multiply_convert_fusion.5
  348.5 3.2 fusion.41
  352.2 22.6 %fusion.18 = bf16[768,2304]{0,1:T(8,128)(2,1)S(1)} fusion(bf16[1024,768]{1,0:T(8,128)(2,1)S(1)} %copy-done.29, bf16[512,768]{0,1:T(8,128)(2,1)S(1)} %bitcast.164, bf16[512,768]{0,1:T(8,128)(2,1)} %bitcast.155, bf16[512,768]{0,1:T(8,128)(2,1)S(1)} %bitcast.153, bf16[512,768]{0,1:T(8,128)(2,1)S(1)} %bitcast.161, bf16[512,768]{0,1:T(8,128)(2,1)S(1)} %bitcast.149, ...), kind=kOutput, calls=%fused_computation.39 | convolution fusion | flops 3653959680 | bytes 9830400 | tf_op jit(solution)/shard_map/td,tc->dc/dot_general | solution.py:210
  394.0 3.1 pad_maximum_fusion.2
  398.5 9.8 %convolution_convert_fusion = bf16[3072,768]{1,0:T(8,128)(2,1)} fusion(bf16[1024,3072]{1,0:T(8,128)(2,1)} %get-tuple-element.111, bf16[1024,768]{0,1:T(8,128)(2,1)S(1)} %copy-done.31), kind=kOutput, calls=%fused_computation.34 | convolution fusion | flops 4834197504 | bytes 12582912 | tf_op jit(solution)/shard_map/tf,td->fd/dot_general | solution.py:178
  408.4 5.1 convolution_convert_fusion.4
  413.4 2.4 copy.99
  415.9 8.6 %convolution_convert_fusion.1 = bf16[768,3072]{1,0:T(8,128)(2,1)S(1)} fusion(bf16[1024,3072]{1,0:T(8,128)(2,1)} %get-tuple-element.121, f32[1024,768]{0,1:T(8,128)S(1)} %copy-done.4, f32[768]{0:T(1024)S(1)} %copy-done.37, f32[768]{0:T(1024)S(1)} %reshape.426, f32[1024]{0:T(1024)S(1)} %copy-done.35, f32[1024]{0:T(1024)S(1)} %broadcast_multiply_fusion.5), kind=kOutput, calls=%fused_computation.35 | convolution fusion | flops 4838129664 | bytes 14170112 | tf_op jit(solution)/shard_map/td,tf->df/dot_general | solution.py:183
  424.5 2.9 pad_maximum_fusion
  427.5 1.9 copy-done.22
  429.4 8.8 %fusion.32 = f32[1024,768]{0,1:T(8,128)} fusion(f32[1024,768]{0,1:T(8,128)S(1)} %copy-done.22, bf16[768,2432]{1,0:T(8,128)(2,1)} %bitcast.138, bf16[512,768]{0,1:T(8,128)(2,1)} %bitcast.165, bf16[512,768]{0,1:T(8,128)(2,1)} %bitcast.156, bf16[512,768]{0,1:T(8,128)(2,1)} %bitcast.151, bf16[512,768]{0,1:T(8,128)(2,1)} %bitcast.160, ...), kind=kOutput, calls=%fused_computation.75 | convolution fusion | flops 3652976640 | bytes 14548992 | tf_op jit(solution)/shard_map/tc,dc->td/dot_general | solution.py:231
  438.2 3.7 copy.101
  443.5 95.3 %all-reduce.5.cloned.1.call-done = bf16[768,2432]{0,1:T(8,128)(2,1)} async-done(((bf16[768,2432]{0,1:T(8,128)(2,1)}), bf16[768,2432]{0,1:T(8,128)(2,1)}) %all-reduce.5.cloned.1.call-update) | async-done | bytes 3735568
  544.1 106.9 %reduce-scatter.6.cloned.1.call-done = bf16[96,768]{1,0:T(8,128)(2,1)} async-done(((bf16[3072,768]{1,0:T(8,128)(2,1)}), bf16[96,768]{1,0:T(8,128)(2,1)}) %reduce-scatter.6.cloned.1.call-update) | async-done | bytes 147472 | tf_op jit(solution)/shard_map/reduce_scatter | solution.py:179
  652.6 116.2 %reduce-scatter.4.cloned.1.call-done = bf16[24,3840]{1,0:T(8,128)(2,1)} async-done(((bf16[768,3840]{1,0:T(8,128)(2,1)}), bf16[24,3840]{1,0:T(8,128)(2,1)}) %reduce-scatter.4.cloned.1.call-update) | async-done | bytes 184336 | tf_op jit(solution)/shard_map/reduce_scatter | solution.py:189
  (206 shorter events, 62.0 us)
Async XLA Ops:
  7.2 227.7 %all-gather.3.cloned.1.call-start = ((), (), s32[]{:S(2)}) async-start(), calls=%async_computation.2 | async-start | bytes 6082560 | tf_op jit(solution)/shard_map/all_gather | solution.py:145
  8.8 242.6 %all-gather.5.cloned.1.call-start = ((), (), s32[]{:S(2)}) async-start(), calls=%async_computation.3 | async-start | bytes 4866048 | tf_op jit(solution)/shard_map/all_gather | solution.py:150
  15.3 1.5 collective-permute-start
  16.9 9.7 %collective-permute-start.1 = (bf16[2,24,2432]{2,1,0:T(8,128)(2,1)S(1)}, bf16[2,24,2432]{2,1,0:T(8,128)(2,1)S(1)}, u32[]{:S(2)}, u32[]{:S(2)}) collective-permute-start(bf16[2,24,2432]{2,1,0:T(8,128)(2,1)S(1)} %get-tuple-element.78), channel_id=1, source_target_pairs={{0,2},{1,3},{2,0},{3,1},{4,6},{5,7},{6,4},{7,5},{8,10},{9,11},{10,... | collective-permute-start | bytes 700424 | tf_op jit(solution)/shard_map/ppermute | solution.py:26
  26.8 11.4 %collective-permute-start.2 = (bf16[4,24,2432]{2,1,0:T(8,128)(2,1)S(1)}, bf16[4,24,2432]{2,1,0:T(8,128)(2,1)S(1)}, u32[]{:S(2)}, u32[]{:S(2)}) collective-permute-start(bf16[4,24,2432]{2,1,0:T(8,128)(2,1)S(1)} %bitcast.157), channel_id=1, source_target_pairs={{0,4},{1,5},{2,6},{3,7},{4,0},{5,1},{6,2},{7,3},{8,12},{9,13},{10,... | collective-permute-start | bytes 1400840 | tf_op jit(solution)/shard_map/ppermute | solution.py:26
  38.5 29.7 %collective-permute-start.3 = (bf16[8,24,2432]{2,1,0:T(8,128)(2,1)S(1)}, bf16[8,24,2432]{2,1,0:T(8,128)(2,1)S(1)}, u32[]{:S(2)}, u32[]{:S(2)}) collective-permute-start(bf16[8,24,2432]{2,1,0:T(8,128)(2,1)S(1)} %bitcast.139), channel_id=1, source_target_pairs={{0,8},{1,9},{2,10},{3,11},{4,12},{5,13},{6,14},{7,15},{8,0},{9,1},... | collective-permute-start | bytes 2801672 | tf_op jit(solution)/shard_map/ppermute | solution.py:26
  68.2 5.9 copy-start.40
  68.4 5.8 copy-start.27
  68.7 10.8 %copy-start.38 = (s32[4,512]{1,0:T(4,128)S(1)}, s32[4,512]{1,0:T(4,128)}, u32[]{:S(2)}) copy-start(s32[4,512]{1,0:T(4,128)} %param.18) | copy-start | bytes 24580
  68.7 97.8 %collective-permute-start.4 = (bf16[16,24,2432]{2,1,0:T(8,128)(2,1)S(1)}, bf16[16,24,2432]{2,1,0:T(8,128)(2,1)}, u32[]{:S(2)}, u32[]{:S(2)}) collective-permute-start(bf16[16,24,2432]{2,1,0:T(8,128)(2,1)S(1)} %bitcast.134), channel_id=1, source_target_pairs={{0,16},{1,17},{2,18},{3,19},{4,20},{5,21},{6,22},{7,23},{8,24},{9,... | collective-permute-start | bytes 5603336 | tf_op jit(solution)/shard_map/ppermute | solution.py:26
  74.0 464.8 %all-reduce.5.cloned.1.call-start = ((), (), s32[]{:S(2)}) async-start(), calls=%async_computation.6 | async-start | bytes 7471104
  188.5 12.6 %copy-start.6 = (pred[512,512]{0,1:T(8,128)(4,1)S(1)}, pred[512,512]{0,1:T(8,128)(4,1)}, u32[]{:S(2)}) copy-start(pred[512,512]{0,1:T(8,128)(4,1)} %fusion.47) | copy-start | bytes 786436
  203.2 4.5 copy-start
  203.2 5.2 copy-start.5
  208.1 43.3 %copy-start.36 = (f32[768]{0:T(1024)}, f32[768]{0:T(1024)S(1)}, u32[]{:S(2)}) copy-start(f32[768]{0:T(1024)S(1)} %reshape.427) | copy-start | bytes 9220
  208.4 16.1 %slice-start = ((s8[12582912]{0:T(1024)(128)(4,1)}), s8[4194304]{0:T(1024)(128)(4,1)S(1)}, s32[]{:S(2)}) async-start(s8[12582912]{0:T(1024)(128)(4,1)} %bitcast.128), calls=%async_computation.7 | async-start | bytes 8388608
  208.4 16.1 %slice-start.1 = ((s8[12582912]{0:T(1024)(128)(4,1)}), s8[4194304]{0:T(1024)(128)(4,1)S(1)}, s32[]{:S(2)}) async-start(s8[12582912]{0:T(1024)(128)(4,1)} %bitcast.128), calls=%async_computation.8 | async-start | bytes 8388608
  217.2 7.3 slice-start.2
  224.5 5.9 copy-start.1
  224.6 5.9 copy-start.16
  230.4 4.5 copy-start.41
  234.9 5.4 copy-start.39
  240.3 54.5 %copy-start.34 = (f32[1024]{0:T(1024)}, f32[1024]{0:T(1024)S(1)}, u32[]{:S(2)}) copy-start(f32[1024]{0:T(1024)S(1)} %add_rsqrt_fusion.1) | copy-start | bytes 12292
  260.9 6.2 slice-start.9
  261.3 5.8 slice-start.10
  267.1 16.3 %copy-start.30 = (bf16[1024,768]{0,1:T(8,128)(2,1)}, bf16[1024,768]{0,1:T(8,128)(2,1)S(1)}, u32[]{:S(2)}) copy-start(bf16[1024,768]{0,1:T(8,128)(2,1)S(1)} %get-tuple-element.65) | copy-start | bytes 4718596
  267.1 16.3 %copy-start.3 = (f32[1024,768]{0,1:T(8,128)S(1)}, f32[1024,768]{0,1:T(8,128)}, u32[]{:S(2)}) copy-start(f32[1024,768]{0,1:T(8,128)} %copy-done.2) | copy-start | bytes 9437188
  267.1 34.0 %slice-start.3 = ((s8[12582912]{0:T(1024)(128)(4,1)}), s8[4194304]{0:T(1024)(128)(4,1)S(1)}, s32[]{:S(2)}) async-start(s8[12582912]{0:T(1024)(128)(4,1)} %bitcast.130), calls=%async_computation.10 | async-start | bytes 8388608
  267.1 34.0 %slice-start.4 = ((s8[12582912]{0:T(1024)(128)(4,1)}), s8[4194304]{0:T(1024)(128)(4,1)S(1)}, s32[]{:S(2)}) async-start(s8[12582912]{0:T(1024)(128)(4,1)} %bitcast.130), calls=%async_computation.11 | async-start | bytes 8388608
  283.4 17.8 %slice-start.5 = ((s8[12582912]{0:T(1024)(128)(4,1)}), s8[4194304]{0:T(1024)(128)(4,1)S(1)}, s32[]{:S(2)}) async-start(s8[12582912]{0:T(1024)(128)(4,1)} %bitcast.130), calls=%async_computation.12 | async-start | bytes 8388608
  301.1 7.2 copy-start.19
  308.3 7.5 copy-start.12
  320.8 3.9 copy-start.17
  324.7 11.2 %slice-start.6 = ((s8[12582912]{0:T(1024)(128)(4,1)}), s8[4194304]{0:T(1024)(128)(4,1)S(1)}, s32[]{:S(2)}) async-start(s8[12582912]{0:T(1024)(128)(4,1)} %bitcast.132), calls=%async_computation.13 | async-start | bytes 8388608
  324.7 11.2 %slice-start.7 = ((s8[12582912]{0:T(1024)(128)(4,1)}), s8[4194304]{0:T(1024)(128)(4,1)S(1)}, s32[]{:S(2)}) async-start(s8[12582912]{0:T(1024)(128)(4,1)} %bitcast.132), calls=%async_computation.14 | async-start | bytes 8388608
  324.7 12.6 %slice-start.8 = ((s8[12582912]{0:T(1024)(128)(4,1)}), s8[4194304]{0:T(1024)(128)(4,1)S(1)}, s32[]{:S(2)}) async-start(s8[12582912]{0:T(1024)(128)(4,1)} %bitcast.132), calls=%async_computation.15 | async-start | bytes 8388608
  337.3 7.1 copy-start.8
  348.5 3.7 copy-start.23
  348.5 3.7 copy-start.24
  348.5 3.7 copy-start.29
  351.7 23.1 %copy-start.33 = (bf16[12,64,512]{2,1,0:T(8,128)(2,1)}, bf16[12,64,512]{2,1,0:T(8,128)(2,1)S(1)}, u32[]{:S(2)}) copy-start(bf16[12,64,512]{2,1,0:T(8,128)(2,1)S(1)} %fusion.41) | copy-start | bytes 2359300
  397.1 253.9 %reduce-scatter.6.cloned.1.call-start = ((), (), s32[]{:S(2)}) async-start(), calls=%async_computation.5 | async-start | bytes 4866048 | tf_op jit(solution)/shard_map/reduce_scatter | solution.py:179
  408.3 7.6 copy-start.4
  408.3 7.6 copy-start.35
  408.3 7.5 copy-start.37
  408.3 360.5 %reduce-scatter.4.cloned.1.call-start = ((), (), s32[]{:S(2)}) async-start(), calls=%async_computation.4 | async-start | bytes 6082560 | tf_op jit(solution)/shard_map/reduce_scatter | solution.py:189
  415.9 8.6 %copy-start.14 = (bf16[768,768]{1,0:T(8,128)(2,1)S(1)}, bf16[768,768]{1,0:T(8,128)(2,1)}, u32[]{:S(2)}) copy-start(bf16[768,768]{1,0:T(8,128)(2,1)} %copy.99) | copy-start | bytes 3538948
  438.2 3.7 copy-start.13
  (15 other events, 36.0 us)
Sparse Core Ops, SparseCore 0:
  11.5 120.5 all-gather.2
  135.0 76.7 all-gather.4
  397.2 141.5 all-reduce.4
  544.1 106.8 reduce-scatter.5
  656.5 112.2 reduce-scatter.3
